TPU v7x, 256 devices: a whole 4x4x8 slice. The times are simulated.
256 devices in a mesh: ctx: 64 (over x, z_hi, y), head: 4 (over z_lo, core).
Axes of the slice: x: 4, y: 4, z: 8 (z_hi: 4, z_lo: 2; z = z_hi * 2 + z_lo), core: 2. Of those that a mesh axis runs over, the one named last changes fastest.
Arguments:
- hidden_in: bfloat16 [2, 32768, 2048], P(None, 'ctx', 'head'), may hold values from -6 to 6
- projected: bfloat16 [3, 2, 32768, 2048], P(None, None, 'ctx', 'head'), may hold values from -4.5 to 4.5
- w_out: bfloat16 [2048, 2048], P(None, 'head'), may hold values from -0.125 to 0.125
- fast_up: bfloat16 [2, 4, 512, 512], P(None, 'head'), may hold values from -0.25 to 0.25
- fast_down: bfloat16 [4, 512, 512], P('head'), may hold values from -0.25 to 0.25
- learn_rates: float32 [4, 2, 32768], P('head', None, 'ctx'), may hold values from 0.02 to 0.2
Outputs:
- layer_out: bfloat16 [2, 32768, 2048], P(None, 'ctx', 'head')
- fast_up_final: float32 [2, 4, 512, 512], P(None, 'head')
- fast_down_final: float32 [4, 512, 512], P('head')
All inputs are finite; a program needn't handle non-finite values.
Results may differ from a plain program's by a relative error of at most 0.0087.
Values may be sent and summed in bfloat16 or wider, within the bound.
A program may use at most 128 MiB of HBM per device.

v0:
```python
import math

import jax
import jax.numpy as jnp
from jax import lax
from jax.sharding import PartitionSpec as P

HD = 128
WIN = 512


def shifted(shard, axis, by):
    peers = lax.axis_size(axis)
    return lax.ppermute(shard, axis, [(i, (i + by) % peers) for i in range(peers)])


def fast_apply(rows_in, w_one, w_three, w_two):
    pre_gate = jnp.dot(rows_in, w_one, preferred_element_type=jnp.float32)
    pre_up = jnp.dot(rows_in, w_three, preferred_element_type=jnp.float32)
    hidden = (pre_gate * jax.nn.sigmoid(pre_gate) * pre_up).astype(jnp.bfloat16)
    result = jnp.dot(hidden, w_two, preferred_element_type=jnp.float32)
    return result * lax.rsqrt(jnp.mean(result * result, axis=-1, keepdims=True) + 1e-05)


def fast_grads(key_rows, value_rows, step_size, w_one, w_three, w_two):
    pre_gate = jnp.dot(key_rows, w_one, preferred_element_type=jnp.float32)
    pre_up = jnp.dot(key_rows, w_three, preferred_element_type=jnp.float32)
    gate_sig = jax.nn.sigmoid(pre_gate)
    hidden = (pre_gate * gate_sig * pre_up).astype(jnp.bfloat16)
    out_grad = (-step_size[:, None] * value_rows.astype(jnp.float32)).astype(jnp.bfloat16)
    grad_two = jnp.einsum("tf,tg->fg", hidden, out_grad, preferred_element_type=jnp.float32)
    hidden_grad = jnp.einsum("tg,fg->tf", out_grad, w_two, preferred_element_type=jnp.float32)
    gate_grad = (hidden_grad * pre_up * gate_sig * (1.0 + pre_gate * (1.0 - gate_sig))).astype(
        jnp.bfloat16
    )
    up_grad = (hidden_grad * pre_gate * gate_sig).astype(jnp.bfloat16)
    grad_one = jnp.einsum("tf,tg->fg", key_rows, gate_grad, preferred_element_type=jnp.float32)
    grad_three = jnp.einsum("tf,tg->fg", key_rows, up_grad, preferred_element_type=jnp.float32)
    return (grad_one, grad_three, grad_two)


def renorm(old_weight, gradient):
    moved_weight = old_weight - gradient
    return moved_weight * (
        jnp.sqrt(jnp.sum(old_weight * old_weight))
        / jnp.sqrt(jnp.sum(moved_weight * moved_weight) + 1e-06)
    )


def update_weights(weights_now, gradients):
    summed = lax.psum((gradients[0], gradients[1], gradients[2]), "ctx")
    return (
        renorm(weights_now[0], summed[0]),
        renorm(weights_now[1], summed[1]),
        renorm(weights_now[2], summed[2]),
    )


def body(hidden_in, projected, w_out, fast_up, fast_down, learn_rates):
    block_count, tok_rows, feat_dim = hidden_in.shape
    ctx_index = lax.axis_index("ctx")
    block_len = tok_rows * lax.axis_size("ctx")
    queries = projected[0]
    key_own = projected[1]
    value_own = projected[2]
    key_prev, value_prev = shifted((key_own, value_own), "ctx", 1)
    at_start = ctx_index == 0
    key_lower = jnp.concatenate([key_prev[:1], key_prev[:-1]], axis=0)
    value_lower = jnp.concatenate([value_prev[:1], value_prev[:-1]], axis=0)
    key_before = jnp.where(at_start, key_lower, key_prev)
    value_before = jnp.where(at_start, value_lower, value_prev)
    head_count = feat_dim // HD
    key_all = jnp.concatenate([key_before, key_own], axis=1).reshape(
        block_count, 2 * tok_rows, head_count, HD
    )
    value_all = jnp.concatenate([value_before, value_own], axis=1).reshape(
        block_count, 2 * tok_rows, head_count, HD
    )
    query_heads = queries.reshape(block_count, tok_rows, head_count, HD)
    scores = jnp.einsum(
        "cqhd,ckhd->chqk", query_heads, key_all, preferred_element_type=jnp.float32
    ) * (1.0 / math.sqrt(HD))
    row_ids = jnp.arange(tok_rows, dtype=jnp.int32)[:, None]
    col_ids = jnp.arange(2 * tok_rows, dtype=jnp.int32)[None, :]
    distance = row_ids + tok_rows - col_ids
    prev_usable = (ctx_index > 0) | (jnp.arange(block_count, dtype=jnp.int32) > 0)
    allowed = ((distance >= 0) & (distance < WIN))[None] & (
        (col_ids >= tok_rows)[None] | prev_usable[:, None, None]
    )
    scores = jnp.where(allowed[:, None], scores, -1e30)
    row_peak = jnp.max(scores, axis=-1, keepdims=True)
    lifted = jnp.exp(scores - row_peak)
    weights = (lifted / jnp.sum(lifted, axis=-1, keepdims=True)).astype(jnp.bfloat16)
    attended = jnp.einsum("chqk,ckhd->cqhd", weights, value_all, preferred_element_type=jnp.float32)
    attended = attended.astype(jnp.bfloat16).reshape(block_count, tok_rows, feat_dim)
    weights_now = (
        fast_up[0, 0].astype(jnp.float32),
        fast_up[1, 0].astype(jnp.float32),
        fast_down[0].astype(jnp.float32),
    )
    step_scale = 1.0 / math.sqrt(block_len)
    mixed_rows = []
    for block_idx in range(block_count):
        w_one = weights_now[0].astype(jnp.bfloat16)
        w_three = weights_now[1].astype(jnp.bfloat16)
        w_two = weights_now[2].astype(jnp.bfloat16)
        fast_out = fast_apply(queries[block_idx], w_one, w_three, w_two)
        mixed_rows.append((attended[block_idx].astype(jnp.float32) + fast_out).astype(jnp.bfloat16))
        gradients = fast_grads(
            key_own[block_idx],
            value_own[block_idx],
            learn_rates[0, block_idx] * step_scale,
            w_one,
            w_three,
            w_two,
        )
        weights_now = update_weights(weights_now, gradients)
    mixed = jnp.stack(mixed_rows)
    projected_out = jnp.einsum(
        "ctf,fg->ctg",
        lax.all_gather(mixed, "head", axis=2, tiled=True),
        w_out,
        preferred_element_type=jnp.float32,
    )
    layer_out = (hidden_in.astype(jnp.float32) + projected_out).astype(jnp.bfloat16)
    fast_up_final = jnp.stack([weights_now[0], weights_now[1]])[:, None]
    fast_down_final = weights_now[2][None]
    return (layer_out, fast_up_final, fast_down_final)


def solution(mesh):
    in_specs = (
        P(None, "ctx", "head"),
        P(None, None, "ctx", "head"),
        P(None, "head"),
        P(None, "head", None, None),
        P("head", None, None),
        P("head", None, "ctx"),
    )
    out_specs = (P(None, "ctx", "head"), P(None, "head", None, None), P("head", None, None))
    return jax.shard_map(body, mesh=mesh, in_specs=in_specs, out_specs=out_specs, check_vma=False)
```

profile of v0, /device:TPU:1, one launch (start us, length us, event | category | flops | bytes accessed | tf_op | source)
XLA Modules:
  0.0 1633.5 jit_solution(5500441415589523369)
XLA Ops:
  7.2 3.7 fusion.124
  28.5 2.5 fusion.63
  32.4 3.4 multiply_reduce_fusion.10
  43.9 2.4 broadcast_and_fusion
  46.3 11.8 collective-permute-done
  59.2 35.4 %collective-permute-done.1 = bf16[2,512,512]{1,2,0:T(8,128)(2,1)} collective-permute-done((bf16[2,512,512]{1,2,0:T(8,128)(2,1)}, bf16[2,512,512]{1,2,0:T(8,128)(2,1)}, u32[]{:S(2)}, u32[]{:S(2)}) %collective-permute-start.1) | collective-permute-done | bytes 1048608 | tf_op jit(solution)/shard_map/ppermute | solution.py:14
  99.6 9.6 fusion.9
  109.1 18.3 %fusion.127 = (f32[2,4,512]{2,1,0:T(4,128)S(1)}, f32[2,4,512,1024]{2,3,1,0:T(8,128)}) fusion(f32[2,4,1024,512]{3,2,1,0:T(8,128)} %fusion.9, pred[2,512,1024]{1,2,0:T(8,128)(4,1)} %broadcast_and_fusion), kind=kOutput, calls=%fused_computation.177 | output fusion | flops 25166848 | bytes 34619392 | tf_op jit(solution)/shard_map/sub | solution.py:92
  127.4 629.1 %all-reduce.7.cloned.1.call-done = (f32[512,512]{0,1:T(8,128)}, f32[512,512]{0,1:T(8,128)}, f32[512,512]{1,0:T(8,128)}) async-done(((f32[512,512]{0,1:T(8,128)}, f32[512,512]{0,1:T(8,128)}, f32[512,512]{1,0:T(8,128)}), (f32[512,512]{0,1:T(8,128)}, f32[512,512]{0,1:T(8,128)}, f32[512,512]{1,0:T(8,128)})) %all-reduce.7.cloned.1.call-update) | async-done | bytes 3145744 | tf_op jit(solution)/shard_map/psum | solution.py:51
  756.5 3.9 multiply_reduce_fusion.8
  763.0 3.2 multiply_reduce_fusion.7
  767.5 2.5 convolution_bitcast_fusion.2
  770.0 2.8 convolution_bitcast_fusion.3
  774.8 3.4 fusion.87
  778.2 2.8 convolution_bitcast_fusion.1
  781.0 2.6 convolution_bitcast_fusion
  783.9 7.8 fusion.23
  793.5 2.5 convolution_bitcast_fusion.6
  796.0 4.0 multiply_reduce_fusion.6
  803.7 721.5 %all-reduce.5.cloned.1.call-done = (f32[512,512]{0,1:T(8,128)}, f32[512,512]{0,1:T(8,128)}, f32[512,512]{1,0:T(8,128)}) async-done(((f32[512,512]{0,1:T(8,128)}, f32[512,512]{0,1:T(8,128)}, f32[512,512]{1,0:T(8,128)}), (f32[512,512]{0,1:T(8,128)}, f32[512,512]{0,1:T(8,128)}, f32[512,512]{1,0:T(8,128)})) %all-reduce.5.cloned.1.call-update) | async-done | bytes 3145744 | tf_op jit(solution)/shard_map/psum | solution.py:51
  1532.4 2.4 multiply_reduce_fusion.2
  1539.9 3.0 copy.32
  1545.3 75.9 %all-gather.2.cloned.1.call-done = bf16[2,512,2048]{1,2,0:T(8,128)(2,1)} async-done(((bf16[2,512,512]{1,2,0:T(8,128)(2,1)}), bf16[2,512,2048]{1,2,0:T(8,128)(2,1)}) %all-gather.2.cloned.1.call-update) | async-done | bytes 4194320 | tf_op jit(solution)/shard_map/all_gather | solution.py:121
  1621.2 5.8 add_convert_fusion
  (66 shorter events, 51.3 us)
Async XLA Ops:
  7.2 1614.0 %copy-start = (bf16[2048,512]{1,0:T(8,128)(2,1)S(1)}, bf16[2048,512]{1,0:T(8,128)(2,1)}, u32[]{:S(2)}) copy-start(bf16[2048,512]{1,0:T(8,128)(2,1)} %param.8) | copy-start | bytes 6291460
  7.2 749.3 %all-reduce.7.cloned.1.call-start = ((), (), s32[]{:S(2)}) async-start(), calls=%async_computation.2 | async-start | bytes 6291456 | tf_op jit(solution)/shard_map/psum | solution.py:51
  11.0 8.1 copy-start.4
  13.3 44.8 %collective-permute-start = (bf16[2,512,512]{1,2,0:T(8,128)(2,1)}, bf16[2,512,512]{1,2,0:T(8,128)(2,1)}, u32[]{:S(2)}, u32[]{:S(2)}) collective-permute-start(bf16[2,512,512]{1,2,0:T(8,128)(2,1)} %bitcast.157), channel_id=1, source_target_pairs={{0,4},{4,8},{8,12},{12,16},{16,20},{20,24},{24,28},{28,32},{32,36}... | collective-permute-start | bytes 3145736 | tf_op jit(solution)/shard_map/ppermute | solution.py:14
  15.5 6.6 copy-start.10
  17.8 4.3 copy-start.1
  17.8 4.3 copy-start.6
  17.8 76.8 %collective-permute-start.1 = (bf16[2,512,512]{1,2,0:T(8,128)(2,1)}, bf16[2,512,512]{1,2,0:T(8,128)(2,1)}, u32[]{:S(2)}, u32[]{:S(2)}) collective-permute-start(bf16[2,512,512]{1,2,0:T(8,128)(2,1)} %bitcast.154), channel_id=1, source_target_pairs={{0,4},{4,8},{8,12},{12,16},{16,20},{20,24},{24,28},{28,32},{32,36}... | collective-permute-start | bytes 3145736 | tf_op jit(solution)/shard_map/ppermute | solution.py:14
  27.4 1497.8 %all-reduce.5.cloned.1.call-start = ((), (), s32[]{:S(2)}) async-start(), calls=%async_computation.1 | async-start | bytes 6291456 | tf_op jit(solution)/shard_map/psum | solution.py:51
  774.7 3.4 copy-start.8
  774.7 3.4 copy-start.9
  783.6 837.6 %all-gather.2.cloned.1.call-start = ((), (), s32[]{:S(2)}) async-start(), calls=%async_computation | async-start | bytes 5242880 | tf_op jit(solution)/shard_map/all_gather | solution.py:121
  783.8 8.7 copy-start.7
  1536.2 1.6 copy-start.2
  1536.2 1.8 copy-start.5
  1539.9 3.0 copy-start.3
Sparse Core Ops, SparseCore 0:
  27.5 728.9 all-reduce.6
  783.7 741.4 all-reduce.4
  1527.0 94.1 all-gather.1
where the time goes:
time: 1630 us
  waiting for transfers between devices  1470 us (90%)
  matrix products  59.7 us (4%)
  other arithmetic  48.2 us (3%)
  local copies, waits for them, and re-layouts  26 us (2%)
  between operations  22 us (1%)
    psum x2, waiting for transfers between devices, update_weights(): summed = lax.psum((gradients[0], gradients[1], gradients[2]), 'ctx')  1350 us
    all_gather x1, waiting for transfers between devices, body(): lax.all_gather(mixed, 'head', axis=2, tiled=True)  75.9 us
    ppermute x2, waiting for transfers between devices, shifted(): lax.ppermute(shard, axis, [(i, (i + by) % peers) for i in range(peers)])  47.2 us
  transfers between devices with their start and end apart: 5, of which 5 were waited for; matrix products, arithmetic and copies ran while one was open for 6% of the time, Pallas kernels for 0%

commit v1 on v0

v1 whole, which is shorter than its diff:
```python
import math

import jax
import jax.numpy as jnp
from jax import lax
from jax.experimental import pallas as pl
from jax.experimental.pallas import tpu as pltpu
from jax.sharding import PartitionSpec as P

MESH = pl.DeviceIdType.MESH
F32 = jnp.float32
BF16 = jnp.bfloat16
HD = 128
FD = 512
TOK = 512
HEADS = 4
BLOCKS = 2
BLOCK_LEN = 32768
LANES = 128
COLOURS = 4
SCALE = math.log2(math.e) / math.sqrt(HD)
ORDER = (
    ("x1", "x3", "y1", "y3"),
    ("x3", "x1", "y3", "y1"),
    ("y1", "y3", "x1", "x3"),
    ("y3", "y1", "x3", "x1"),
)


class Place:
    def __init__(self):
        ctx = lax.axis_index("ctx")
        self.head = lax.axis_index("head")
        self.x = ctx // 16
        self.z = (ctx // 4) % 4
        self.y = ctx % 4
        x_low, x_high = self.x % 2, self.x // 2
        y_low, y_high = self.y % 2, self.y // 2
        self.key = {
            "x1": (x_low + x_high) % 2,
            "x3": x_high,
            "y1": (y_low + y_high) % 2,
            "y3": y_high,
        }
        self.partner = {
            "x1": self.at(self.x + 1 - 2 * x_low, self.z, self.y),
            "x3": self.at(3 - self.x, self.z, self.y),
            "y1": self.at(self.x, self.z, self.y + 1 - 2 * y_low),
            "y3": self.at(self.x, self.z, 3 - self.y),
        }
        self.z_peer = [self.at(self.x, (self.z + d) % 4, self.y) for d in (1, 2, 3)]
        self.z_to = [(self.z + d) % 4 for d in (1, 2, 3)]
        self.before = ((ctx + 63) % 64, self.head)
        self.after = ((ctx + 1) % 64, self.head)
        self.sibling = self.head + 1 - 2 * (self.head % 2)
        self.across = (self.head + 2) % 4
        self.diagonal = (self.sibling + 2) % 4
        self.to_sibling = (ctx, self.sibling)
        self.to_across = (ctx, self.across)
        self.first = ctx == 0
        self.last = ctx // 63
        self.keep, self.send, self.mine = [], [], []
        for colour in range(COLOURS):
            keeps, sends, off = [], [], 0
            for step in range(4):
                length = 256 >> step
                key = self.key[ORDER[colour][step]]
                keeps.append(pl.multiple_of(off + key * length, 32))
                sends.append(pl.multiple_of(off + (1 - key) * length, 32))
                off = off + key * length
            self.keep.append(keeps)
            self.send.append(sends)
            self.mine.append(pl.multiple_of(off, 32))

    def at(self, x, z, y):
        return (x * 16 + z * 4 + y, self.head)

    def rows_of(self, colour):
        row = 0
        for which in range(COLOURS):
            row = row + jnp.where(colour == which, self.mine[which], 0)
        return pl.multiple_of(row, 32)


def remote(src, dst, send_sem, recv_sem, other):
    return pltpu.make_async_remote_copy(
        src_ref=src, dst_ref=dst, send_sem=send_sem, recv_sem=recv_sem, device_id=other, device_id_type=MESH
    )


def block_of(ref, matrix, row, length, colour):
    if isinstance(colour, int):
        lanes = pl.ds(colour * LANES, LANES)
    else:
        lanes = pl.ds(pl.multiple_of(colour * LANES, LANES), LANES)
    return ref.at[matrix, pl.ds(row, length), lanes]


def mm(a, b):
    return lax.dot_general(a, b, (((1,), (0,)), ((), ())), preferred_element_type=F32)


def mm_nt(a, b):
    return lax.dot_general(a, b, (((1,), (1,)), ((), ())), preferred_element_type=F32)


def mm_tn(a, b):
    return lax.dot_general(a, b, (((0,), (0,)), ((), ())), preferred_element_type=F32)


def square_sum(value):
    rows = jnp.sum(value * value, axis=0, keepdims=True)
    return jnp.sum(rows, axis=1, keepdims=True)


def layer_kernel(
    hidden_hbm, proj_hbm, wout_hbm, up_hbm, down_hbm, rates,
    out_hbm, moved_hbm, factor_out,
    proj, hidden, wout, state, q_land, o_out, o_land, stat_out, stat_land, attended, mixed, grad, total, moved0, moved1,
    land0, land1, land2, land3, z_land, piece, hid, gate_g, up_g, out_g, out_stage, out_acc,
    load_sem, store_sem, q_send, q_recv, o_send, o_recv, st_send, st_recv, h_send, h_recv,
    s_send, s_recv, z_send, z_recv, g_send, g_recv, zg_send, zg_recv,
):
    place = Place()
    lands = (land0, land1, land2, land3)
    moved = (moved0, moved1)

    loads = [
        pltpu.make_async_copy(proj_hbm.at[1, 0], proj.at[1, 0], load_sem.at[0]),
        pltpu.make_async_copy(proj_hbm.at[2, 0], proj.at[2, 0], load_sem.at[1]),
        pltpu.make_async_copy(up_hbm.at[0, 0], state.at[0], load_sem.at[2]),
        pltpu.make_async_copy(up_hbm.at[1, 0], state.at[1], load_sem.at[3]),
        pltpu.make_async_copy(down_hbm.at[0], state.at[2], load_sem.at[4]),
        pltpu.make_async_copy(proj_hbm.at[0], proj.at[0], load_sem.at[5]),
        pltpu.make_async_copy(proj_hbm.at[1, 1], proj.at[1, 1], load_sem.at[6]),
        pltpu.make_async_copy(proj_hbm.at[2, 1], proj.at[2, 1], load_sem.at[7]),
        pltpu.make_async_copy(wout_hbm, wout, load_sem.at[8]),
        pltpu.make_async_copy(hidden_hbm, hidden, load_sem.at[9]),
    ]
    for load in loads:
        load.start()

    barrier = pltpu.get_barrier_semaphore()
    others = list(place.partner.values()) + place.z_peer
    others += [place.before, place.after, place.to_sibling, place.to_across]
    for other in others:
        pl.semaphore_signal(barrier, inc=1, device_id=other, device_id_type=MESH)
    pl.semaphore_wait(barrier, len(others))

    def q_copy(block, head):
        lanes = pl.ds(head * HD, HD)
        sem = block * HEADS + head
        return remote(
            proj_hbm.at[0, block, :, lanes], q_land.at[block, :, lanes], q_send.at[sem], q_recv.at[sem], place.before
        )

    def o_copy(block, head):
        lanes = pl.ds(head * HD, HD)
        sem = block * HEADS + head
        return remote(
            o_out.at[block, :, lanes], o_land.at[block, :, lanes], o_send.at[sem], o_recv.at[sem], place.after
        )

    def stat_copy(block):
        return remote(stat_out.at[block], stat_land.at[block], st_send.at[block], st_recv.at[block], place.after)

    def head_copy(block, kind):
        owner, to = (
            (place.head, place.to_sibling),
            (place.head, place.to_across),
            (place.across, place.to_sibling),
        )[kind]
        rows = mixed.at[owner, block]
        return remote(rows, rows, h_send.at[block, kind], h_recv.at[block, kind], to)

    def scatter_copy(step, matrix, colour):
        length = 256 >> step
        return remote(
            block_of(grad, matrix, place.send[colour][step], length, colour),
            lands[step].at[matrix, colour],
            s_send.at[step, matrix, colour],
            s_recv.at[step, matrix, colour],
            place.partner[ORDER[colour][step]],
        )

    def z_copy(d, matrix):
        to = place.z_to[d]
        return remote(
            block_of(grad, matrix, place.rows_of(to), 32, to),
            z_land.at[d, matrix],
            z_send.at[d, matrix],
            z_recv.at[d, matrix],
            place.z_peer[d],
        )

    own_row = place.rows_of(place.z)

    def zg_copy(block, d, matrix):
        own = block_of(moved[block], matrix, own_row, 32, place.z)
        return remote(own, own, zg_send.at[d, matrix], zg_recv.at[d, matrix], place.z_peer[d])

    def gather_copy(block, step, matrix, colour):
        kept = block_of(moved[block], matrix, place.keep[colour][step], 256 >> step, colour)
        return remote(
            kept,
            kept,
            g_send.at[step, matrix, colour],
            g_recv.at[step, matrix, colour],
            place.partner[ORDER[colour][step]],
        )

    for block in range(BLOCKS):
        for head in range(HEADS):
            q_copy(block, head).start()

    def key_pass(block, weights, factors):
        step_scale = -1.0 / math.sqrt(BLOCK_LEN)

        def grown(value, which):
            return value if factors is None else value * factors[which]

        rows_per = 256
        for part in range(TOK // rows_per):
            rows = pl.ds(part * rows_per, rows_per)
            key = proj[1, block, rows, :]
            rate = rates[0, block : block + 1, part * rows_per : (part + 1) * rows_per] * step_scale
            rate = jnp.broadcast_to(rate, (LANES, rows_per)).T
            value = proj[2, block, rows, :].astype(F32)
            out_grad = (value * jnp.concatenate([rate] * 4, axis=1)).astype(BF16)
            out_g[rows, :] = out_grad
            gate = grown(mm(key, weights[0]), 0)
            up = grown(mm(key, weights[1]), 1)
            back = grown(mm_nt(out_grad, weights[2]), 2)
            sig = jax.nn.sigmoid(gate)
            gate_sig = gate * sig
            hid[rows, :] = (gate_sig * up).astype(BF16)
            gate_g[rows, :] = (back * up * (sig + gate_sig * (1.0 - sig))).astype(BF16)
            up_g[rows, :] = (back * gate_sig).astype(BF16)
        for matrix in (2, 1, 0):
            if matrix == 2:
                sums = mm_tn(hid[...], out_g[...])
            elif matrix == 1:
                sums = mm_tn(proj[1, block], up_g[...])
            else:
                sums = mm_tn(proj[1, block], gate_g[...])
            total[matrix] = sums
            grad[matrix] = sums.astype(BF16)
            for colour in range(COLOURS):
                scatter_copy(0, matrix, colour).start()

    def reduction(block, old_factors):
        for step in range(4):
            length = 256 >> step
            for matrix in (2, 1, 0):
                for colour in range(COLOURS):
                    scatter_copy(step, matrix, colour).wait_recv()
                    row = place.keep[colour][step]
                    kept = block_of(total, matrix, row, length, colour)
                    value = kept[...] + lands[step][matrix, colour].astype(F32)
                    kept[...] = value
                    block_of(grad, matrix, row, length, colour)[...] = value.astype(BF16)
                    if step < 3:
                        scatter_copy(step + 1, matrix, colour).start()
                if step == 3:
                    for d in range(3):
                        z_copy(d, matrix).start()
                yield
        for matrix in (2, 1, 0):
            value = block_of(total, matrix, own_row, 32, place.z)[...]
            for d in range(3):
                z_copy(d, matrix).wait_recv()
                value = value + z_land[d, matrix].astype(F32)
            if block == 0:
                value = block_of(state, matrix, own_row, 32, place.z)[...].astype(F32) - value
                piece[matrix] = value
            else:
                value = piece[matrix] * old_factors[matrix] - value
            block_of(moved[block], matrix, own_row, 32, place.z)[...] = value.astype(BF16)
            for d in range(3):
                zg_copy(block, d, matrix).start()
            yield
        for step in (3, 2, 1, 0):
            for matrix in (2, 1, 0):
                if step == 3:
                    for d in range(3):
                        zg_copy(block, d, matrix).wait_recv()
                for colour in range(COLOURS):
                    if step < 3:
                        gather_copy(block, step + 1, matrix, colour).wait_recv()
                    gather_copy(block, step, matrix, colour).start()
                yield
        for matrix in (2, 1, 0):
            for colour in range(COLOURS):
                gather_copy(block, 0, matrix, colour).wait_recv()
        for matrix in range(3):
            for colour in range(COLOURS):
                for step in range(4):
                    scatter_copy(step, matrix, colour).wait_send()
                    gather_copy(block, step, matrix, colour).wait_send()
            for d in range(3):
                z_copy(d, matrix).wait_send()
                zg_copy(block, d, matrix).wait_send()

    tile_row = lax.broadcasted_iota(jnp.int32, (HD, HD), 0)
    tile_col = lax.broadcasted_iota(jnp.int32, (HD, HD), 1)

    def softmax_part(scores, values):
        peak = jnp.max(scores, axis=1, keepdims=True)
        lifted = jnp.exp2((scores - peak) * SCALE)
        weight = jnp.sum(lifted, axis=1, keepdims=True)
        return mm(lifted.astype(BF16), values), peak * SCALE, weight

    def masked(scores, keep, last):
        width = scores.shape[1]
        if width == HD:
            return jnp.where(keep, scores, -1e30)
        if last:
            return jnp.concatenate([scores[:, : width - HD], jnp.where(keep, scores[:, width - HD :], -1e30)], axis=1)
        return jnp.concatenate([jnp.where(keep, scores[:, :HD], -1e30), scores[:, HD:]], axis=1)

    def far_item(block, head):
        lanes = pl.ds(head * HD, HD)
        q_copy(block, head).wait_recv()
        source = jnp.maximum(block - place.last, 0)
        for tile in range(4):
            rows = pl.ds(tile * HD, HD)
            span = pl.ds(tile * HD, TOK - tile * HD)
            scores = mm_nt(q_land[block, rows, lanes], proj[1, source, span, lanes])
            scores = masked(scores, tile_col > tile_row, False)
            result, peak, weight = softmax_part(scores, proj[2, source, span, lanes])
            o_out[block, rows, lanes] = (result / weight).astype(BF16)
            log_sum = jnp.broadcast_to(peak + jnp.log2(weight), (HD, LANES)).T
            stat_out[block, head : head + 1, rows] = log_sum[:1]
        o_copy(block, head).start()
        if head == HEADS - 1:
            stat_copy(block).start()

    def near_item(block, head):
        lanes = pl.ds(head * HD, HD)
        o_copy(block, head).wait_recv()
        if head == 0:
            stat_copy(block).wait_recv()
        for tile in range(4):
            rows = pl.ds(tile * HD, HD)
            span = pl.ds(0, (tile + 1) * HD)
            scores = mm_nt(proj[0, block, rows, lanes], proj[1, block, span, lanes])
            scores = masked(scores, tile_col <= tile_row, True)
            result, peak, weight = softmax_part(scores, proj[2, block, span, lanes])
            far_log = jnp.broadcast_to(stat_land[block, head : head + 1, rows], (LANES, HD)).T
            if block == 0:
                far_log = jnp.where(place.first, -1e30, far_log)
            top = jnp.maximum(peak, far_log)
            near_w = jnp.exp2(peak - top)
            far_w = jnp.exp2(far_log - top)
            far = o_land[block, rows, lanes].astype(F32)
            merged = (result * near_w + far * far_w) / (weight * near_w + far_w)
            attended[block, rows, lanes] = merged.astype(BF16)

    def query_part(block, weights, factors, part):
        rows = pl.ds(part * 256, 256)
        query = proj[0, block, rows, :]
        gate = mm(query, weights[0])
        up = mm(query, weights[1])
        if factors is not None:
            gate = gate * factors[0]
            up = up * factors[1]
        hidden_q = (gate * jax.nn.sigmoid(gate) * up).astype(BF16)
        result = mm(hidden_q, weights[2])
        if factors is not None:
            result = result * factors[2]
        fast = result * lax.rsqrt(jnp.mean(result * result, axis=1, keepdims=True) + 1e-05)
        mixed[place.head, block, rows, :] = (attended[block, rows, :].astype(F32) + fast).astype(BF16)

    def share(block):
        head_copy(block, 0).start()
        head_copy(block, 1).start()

    def forward(block):
        head_copy(block, 1).wait_recv()
        head_copy(block, 2).start()

    def project(block, turn):
        owner = (place.head, place.across, place.sibling, place.diagonal)[turn]
        if turn == 2:
            head_copy(block, 0).wait_recv()
        if turn == 3:
            head_copy(block, 2).wait_recv()
        product = mm(mixed[owner, block], wout[pl.ds(pl.multiple_of(owner * FD, FD), FD), :])
        if turn == 0:
            out_acc[...] = hidden[block].astype(F32) + product
        elif turn < 3:
            out_acc[...] += product
        else:
            out_stage[block] = (out_acc[...] + product).astype(BF16)
            pltpu.make_async_copy(out_stage.at[block], out_hbm.at[block], store_sem.at[block]).start()

    def run(steps, fillers, every):
        count, place_in = 0, 0
        for _ in steps:
            while place_in < len(fillers) and place_in < (count + 1) * every:
                fillers[place_in]()
                place_in += 1
            count += 1
        for filler in fillers[place_in:]:
            filler()

    for load in loads[:5]:
        load.wait()
    key_pass(0, [state[0], state[1], state[2]], None)
    for load in loads[5:]:
        load.wait()
    fillers = [lambda b=b, h=h: far_item(b, h) for b in range(BLOCKS) for h in range(HEADS)]
    fillers += [lambda h=h: near_item(0, h) for h in range(HEADS)]
    fillers += [lambda p=p: query_part(0, [state[0], state[1], state[2]], None, p) for p in range(2)]
    fillers += [lambda: share(0)]
    fillers += [lambda h=h: near_item(1, h) for h in range(HEADS)]
    run(reduction(0, None), fillers, 0.7)

    norm = []
    factors = []
    for matrix in range(3):
        first = jnp.sqrt(square_sum(state[matrix].astype(F32)))
        second = square_sum(moved0[matrix].astype(F32))
        factors.append(first * lax.rsqrt(second + 1e-06))
        norm.append(jnp.sqrt(second) * factors[matrix])
    key_pass(1, [moved0[0], moved0[1], moved0[2]], factors)
    fillers = [lambda p=p: query_part(1, [moved0[0], moved0[1], moved0[2]], factors, p) for p in range(2)]
    fillers += [lambda: share(1), lambda: forward(0)]
    fillers += [lambda t=t: project(0, t) for t in range(4)]
    fillers += [lambda: forward(1)]
    fillers += [lambda t=t: project(1, t) for t in range(4)]
    run(reduction(1, factors), fillers, 0.5)

    final = pltpu.make_async_copy(moved1, moved_hbm, store_sem.at[2])
    final.start()
    for matrix in range(3):
        last = square_sum(moved1[matrix].astype(F32))
        factor = norm[matrix] * lax.rsqrt(last + 1e-06)
        factor_out[matrix] = jnp.broadcast_to(factor, (8, LANES))
    for block in range(BLOCKS):
        for head in range(HEADS):
            q_copy(block, head).wait_send()
            o_copy(block, head).wait_send()
        stat_copy(block).wait_send()
        for kind in range(3):
            head_copy(block, kind).wait_send()
        pltpu.make_async_copy(out_stage.at[block], out_hbm.at[block], store_sem.at[block]).wait()
    final.wait()


def body(hidden_in, projected, w_out, fast_up, fast_down, learn_rates):
    dma = pltpu.SemaphoreType.DMA
    vmem = pltpu.VMEM
    hbm_spec = pl.BlockSpec(memory_space=pl.ANY)
    vmem_spec = pl.BlockSpec(memory_space=pltpu.VMEM)
    square = (FD, FD)
    layer_out, moved, factor = pl.pallas_call(
        layer_kernel,
        out_shape=(
            jax.ShapeDtypeStruct((BLOCKS, TOK, FD), BF16),
            jax.ShapeDtypeStruct((3, FD, FD), BF16),
            jax.ShapeDtypeStruct((3, 8, LANES), F32),
        ),
        in_specs=[hbm_spec] * 5 + [vmem_spec],
        out_specs=(hbm_spec, hbm_spec, vmem_spec),
        scratch_shapes=[
            vmem((3, BLOCKS, TOK, FD), BF16),
            vmem((BLOCKS, TOK, FD), BF16),
            vmem((4 * FD, FD), BF16),
            vmem((3,) + square, BF16),
            vmem((BLOCKS, TOK, FD), BF16),
            vmem((BLOCKS, TOK, FD), BF16),
            vmem((BLOCKS, TOK, FD), BF16),
            vmem((BLOCKS, 8, TOK), F32),
            vmem((BLOCKS, 8, TOK), F32),
            vmem((BLOCKS, TOK, FD), BF16),
            vmem((4, BLOCKS, TOK, FD), BF16),
            vmem((3,) + square, BF16),
            vmem((3,) + square, F32),
            vmem((3,) + square, BF16),
            vmem((3,) + square, BF16),
            vmem((3, COLOURS, 256, LANES), BF16),
            vmem((3, COLOURS, 128, LANES), BF16),
            vmem((3, COLOURS, 64, LANES), BF16),
            vmem((3, COLOURS, 32, LANES), BF16),
            vmem((3, 3, 32, LANES), BF16),
            vmem((3, 32, LANES), F32),
            vmem(square, BF16),
            vmem(square, BF16),
            vmem(square, BF16),
            vmem(square, BF16),
            vmem((BLOCKS, TOK, FD), BF16),
            vmem(square, F32),
            dma((10,)),
            dma((3,)),
            dma((8,)),
            dma((8,)),
            dma((8,)),
            dma((8,)),
            dma((2,)),
            dma((2,)),
            dma((2, 3)),
            dma((2, 3)),
            dma((4, 3, COLOURS)),
            dma((4, 3, COLOURS)),
            dma((3, 3)),
            dma((3, 3)),
            dma((4, 3, COLOURS)),
            dma((4, 3, COLOURS)),
            dma((3, 3)),
            dma((3, 3)),
        ],
        compiler_params=pltpu.CompilerParams(
            collective_id=0, has_side_effects=True, vmem_limit_bytes=60 << 20
        ),
    )(hidden_in, projected, w_out, fast_up, fast_down, learn_rates)
    finals = moved.astype(F32) * factor[:, :1, :1]
    return (layer_out, finals[:2, None], finals[2:])


def solution(mesh):
    in_specs = (
        P(None, "ctx", "head"),
        P(None, None, "ctx", "head"),
        P(None, "head"),
        P(None, "head", None, None),
        P("head", None, None),
        P("head", None, "ctx"),
    )
    out_specs = (P(None, "ctx", "head"), P(None, "head", None, None), P("head", None, None))
    return jax.shard_map(body, mesh=mesh, in_specs=in_specs, out_specs=out_specs, check_vma=False)
```

time: 1630 us -> 157 us (0.10)
  the two profiles are of different devices: /device:TPU:1 before, /device:TPU:64 now
where the time goes in v1:
time: 157 us; the launch traced here: 156 us
  Pallas kernels  149 us (95%)
  local copies, waits for them, and re-layouts  4.32 us (3%)
  other arithmetic  1.94 us (1%)
    pallas_call x1, Pallas kernels, body(): pl.pallas_call(layer_kernel, out_shape=(jax.ShapeDtypeStruct((BLOCKS, TOK...  149 us

profile of v1, /device:TPU:64, one launch (start us, length us, event | category | flops | bytes accessed | tf_op | source)
XLA Modules:
  0.0 156.4 jit_solution(3389980651158317402)
XLA Ops:
  0.6 149.5 %shard_map.85 = (bf16[2,512,512]{2,1,0:T(8,128)(2,1)}, bf16[3,512,512]{2,1,0:T(8,128)(2,1)}, f32[3,8,128]{2,1,0:T(8,128)}) custom-call(bf16[2,512,512]{2,1,0:T(8,128)(2,1)} %hidden_hbm.1, bf16[3,2,512,512]{3,2,1,0:T(8,128)(2,1)} %proj_hbm.1, bf16[2048,512]{1,0:T(8,128)(2,1)} %wout_hbm.1, bf16[2,1,512,512]{3,2,1,0:T(8,128)(2,1)} %up_hbm.1, ...), custom_call_target="tpu_custom_call" | custom-call | tf_op jit(solution)/shard_map/pallas_call | solution.py:457
  150.1 0.8 slice_reduce_fusion
  150.9 1.9 %convert_multiply_fusion = f32[3,512,512]{2,1,0:T(8,128)S(1)} fusion(bf16[3,512,512]{2,1,0:T(8,128)(2,1)} %get-tuple-element.7, f32[3]{0:T(128)S(1)} %slice_reduce_fusion), kind=kLoop, calls=%fused_computation | loop fusion | flops 1572864 | bytes 4718604 | tf_op jit(solution)/shard_map/mul | solution.py:517
  152.9 0.0 copy-start
  152.9 1.0 slice.13
  153.9 1.5 slice_bitcast_fusion
  155.4 0.0 copy-done
  155.4 1.0 copy.12
Async XLA Ops:
  152.9 2.5 %copy-start = (bf16[2,512,512]{2,1,0:T(8,128)(2,1)S(1)}, bf16[2,512,512]{2,1,0:T(8,128)(2,1)}, u32[]{:S(2)}) copy-start(bf16[2,512,512]{2,1,0:T(8,128)(2,1)} %get-tuple-element.18) | copy-start | bytes 3145732

commit v2 on v1

--- a/solution.py
+++ b/solution.py
@@ -115,7 +115,7 @@
 
 def layer_kernel(
     hidden_hbm, proj_hbm, wout_hbm, up_hbm, down_hbm, rates,
-    out_hbm, moved_hbm, factor_out,
+    out_hbm, up_out, down_out, factor_out,
     proj, hidden, wout, state, q_land, o_out, o_land, stat_out, stat_land, attended, mixed, grad, total, moved0, moved1,
     land0, land1, land2, land3, z_land, piece, hid, gate_g, up_g, out_g, out_stage, out_acc,
     load_sem, store_sem, q_send, q_recv, o_send, o_recv, st_send, st_recv, h_send, h_recv,
@@ -147,18 +147,18 @@
         pl.semaphore_signal(barrier, inc=1, device_id=other, device_id_type=MESH)
     pl.semaphore_wait(barrier, len(others))
 
-    def q_copy(block, head):
-        lanes = pl.ds(head * HD, HD)
-        sem = block * HEADS + head
+    def q_copy(block, head, tile):
+        lanes, rows = pl.ds(head * HD, HD), pl.ds(tile * HD, HD)
+        sem = (block * HEADS + head) * 4 + tile
         return remote(
-            proj_hbm.at[0, block, :, lanes], q_land.at[block, :, lanes], q_send.at[sem], q_recv.at[sem], place.before
+            proj_hbm.at[0, block, rows, lanes], q_land.at[block, rows, lanes], q_send.at[sem], q_recv.at[sem], place.before
         )
 
-    def o_copy(block, head):
-        lanes = pl.ds(head * HD, HD)
-        sem = block * HEADS + head
+    def o_copy(block, head, tile):
+        lanes, rows = pl.ds(head * HD, HD), pl.ds(tile * HD, HD)
+        sem = (block * HEADS + head) * 4 + tile
         return remote(
-            o_out.at[block, :, lanes], o_land.at[block, :, lanes], o_send.at[sem], o_recv.at[sem], place.after
+            o_out.at[block, rows, lanes], o_land.at[block, rows, lanes], o_send.at[sem], o_recv.at[sem], place.after
         )
 
     def stat_copy(block):
@@ -209,9 +209,14 @@
             place.partner[ORDER[colour][step]],
         )
 
-    for block in range(BLOCKS):
-        for head in range(HEADS):
-            q_copy(block, head).start()
+    q_copy(0, 0, 0).start()
+    q_copy(0, 0, 1).start()
+    q_copy(0, 0, 2).start()
+    q_copy(0, 0, 3).start()
+    q_copy(0, 1, 0).start()
+    q_copy(0, 1, 1).start()
+    q_copy(0, 1, 2).start()
+    q_copy(0, 1, 3).start()
 
     def key_pass(block, weights, factors):
         step_scale = -1.0 / math.sqrt(BLOCK_LEN)
@@ -318,26 +323,26 @@
             return jnp.concatenate([scores[:, : width - HD], jnp.where(keep, scores[:, width - HD :], -1e30)], axis=1)
         return jnp.concatenate([jnp.where(keep, scores[:, :HD], -1e30), scores[:, HD:]], axis=1)
 
-    def far_item(block, head):
+    def far_tile(block, head, tile):
         lanes = pl.ds(head * HD, HD)
-        q_copy(block, head).wait_recv()
+        q_copy(block, head, tile).wait_recv()
         source = jnp.maximum(block - place.last, 0)
-        for tile in range(4):
-            rows = pl.ds(tile * HD, HD)
-            span = pl.ds(tile * HD, TOK - tile * HD)
-            scores = mm_nt(q_land[block, rows, lanes], proj[1, source, span, lanes])
-            scores = masked(scores, tile_col > tile_row, False)
-            result, peak, weight = softmax_part(scores, proj[2, source, span, lanes])
-            o_out[block, rows, lanes] = (result / weight).astype(BF16)
-            log_sum = jnp.broadcast_to(peak + jnp.log2(weight), (HD, LANES)).T
-            stat_out[block, head : head + 1, rows] = log_sum[:1]
-        o_copy(block, head).start()
-        if head == HEADS - 1:
+        rows = pl.ds(tile * HD, HD)
+        span = pl.ds(tile * HD, TOK - tile * HD)
+        scores = mm_nt(q_land[block, rows, lanes], proj[1, source, span, lanes])
+        scores = masked(scores, tile_col > tile_row, False)
+        result, peak, weight = softmax_part(scores, proj[2, source, span, lanes])
+        o_out[block, rows, lanes] = (result / weight).astype(BF16)
+        log_sum = jnp.broadcast_to(peak + jnp.log2(weight), (HD, LANES)).T
+        stat_out[block, head : head + 1, rows] = log_sum[:1]
+        o_copy(block, head, tile).start()
+        if head == HEADS - 1 and tile == 3:
             stat_copy(block).start()
 
     def near_item(block, head):
         lanes = pl.ds(head * HD, HD)
-        o_copy(block, head).wait_recv()
+        for tile in range(4):
+            o_copy(block, head, tile).wait_recv()
         if head == 0:
             stat_copy(block).wait_recv()
         for tile in range(4):
@@ -394,14 +399,12 @@
             out_stage[block] = (out_acc[...] + product).astype(BF16)
             pltpu.make_async_copy(out_stage.at[block], out_hbm.at[block], store_sem.at[block]).start()
 
-    def run(steps, fillers, every):
-        count, place_in = 0, 0
-        for _ in steps:
-            while place_in < len(fillers) and place_in < (count + 1) * every:
-                fillers[place_in]()
-                place_in += 1
-            count += 1
-        for filler in fillers[place_in:]:
+    def run(steps, fillers):
+        fillers = list(fillers)
+        for count, _ in enumerate(steps):
+            while fillers and fillers[0][0] <= count:
+                fillers.pop(0)[1]()
+        for _, filler in fillers:
             filler()
 
     for load in loads[:5]:
@@ -409,12 +412,62 @@
     key_pass(0, [state[0], state[1], state[2]], None)
     for load in loads[5:]:
         load.wait()
-    fillers = [lambda b=b, h=h: far_item(b, h) for b in range(BLOCKS) for h in range(HEADS)]
-    fillers += [lambda h=h: near_item(0, h) for h in range(HEADS)]
-    fillers += [lambda p=p: query_part(0, [state[0], state[1], state[2]], None, p) for p in range(2)]
-    fillers += [lambda: share(0)]
-    fillers += [lambda h=h: near_item(1, h) for h in range(HEADS)]
-    run(reduction(0, None), fillers, 0.7)
+    fillers = [
+        (0, lambda: far_tile(0, 0, 0)),
+        (0, lambda: far_tile(0, 0, 1)),
+        (0, lambda: far_tile(0, 0, 2)),
+        (0, lambda: q_copy(0, 2, 0).start()),
+        (1, lambda: far_tile(0, 0, 3)),
+        (1, lambda: q_copy(0, 2, 1).start()),
+        (2, lambda: far_tile(0, 1, 0)),
+        (2, lambda: q_copy(0, 2, 2).start()),
+        (3, lambda: far_tile(0, 1, 1)),
+        (3, lambda: q_copy(0, 2, 3).start()),
+        (4, lambda: far_tile(0, 1, 2)),
+        (4, lambda: q_copy(0, 3, 0).start()),
+        (5, lambda: far_tile(0, 1, 3)),
+        (5, lambda: q_copy(0, 3, 1).start()),
+        (6, lambda: far_tile(0, 2, 0)),
+        (6, lambda: q_copy(0, 3, 2).start()),
+        (7, lambda: far_tile(0, 2, 1)),
+        (7, lambda: q_copy(0, 3, 3).start()),
+        (8, lambda: far_tile(0, 2, 2)),
+        (8, lambda: q_copy(1, 0, 0).start()),
+        (9, lambda: far_tile(0, 2, 3)),
+        (9, lambda: q_copy(1, 0, 1).start()),
+        (10, lambda: far_tile(0, 3, 0)),
+        (10, lambda: q_copy(1, 0, 2).start()),
+        (11, lambda: far_tile(0, 3, 1)),
+        (11, lambda: q_copy(1, 0, 3).start()),
+        (12, lambda: far_tile(0, 3, 2)),
+        (12, lambda: q_copy(1, 1, 0).start()),
+        (13, lambda: far_tile(0, 3, 3)),
+        (13, lambda: q_copy(1, 1, 1).start()),
+        (14, lambda: far_tile(1, 0, 0)),
+        (14, lambda: q_copy(1, 1, 2).start()),
+        (15, lambda: far_tile(1, 0, 1)),
+        (15, lambda: q_copy(1, 1, 3).start()),
+        (16, lambda: far_tile(1, 0, 2)),
+        (16, lambda: q_copy(1, 2, 0).start()),
+        (17, lambda: far_tile(1, 0, 3)),
+        (17, lambda: q_copy(1, 2, 1).start()),
+        (18, lambda: far_tile(1, 1, 0)),
+        (18, lambda: q_copy(1, 2, 2).start()),
+        (19, lambda: far_tile(1, 1, 1)),
+        (19, lambda: q_copy(1, 2, 3).start()),
+        (20, lambda: far_tile(1, 1, 2)),
+        (20, lambda: q_copy(1, 3, 0).start()),
+        (21, lambda: far_tile(1, 1, 3)),
+        (21, lambda: q_copy(1, 3, 1).start()),
+        (22, lambda: far_tile(1, 2, 0)),
+        (22, lambda: q_copy(1, 3, 2).start()),
+        (23, lambda: far_tile(1, 2, 1)),
+        (23, lambda: q_copy(1, 3, 3).start()),
+        (24, lambda: far_tile(1, 2, 2)),
+        (25, lambda: far_tile(1, 2, 3)),
+        (26, lambda: far_tile(1, 3, 0)),
+    ]
+    run(reduction(0, None), fillers)
 
     norm = []
     factors = []
@@ -424,28 +477,59 @@
         factors.append(first * lax.rsqrt(second + 1e-06))
         norm.append(jnp.sqrt(second) * factors[matrix])
     key_pass(1, [moved0[0], moved0[1], moved0[2]], factors)
-    fillers = [lambda p=p: query_part(1, [moved0[0], moved0[1], moved0[2]], factors, p) for p in range(2)]
-    fillers += [lambda: share(1), lambda: forward(0)]
-    fillers += [lambda t=t: project(0, t) for t in range(4)]
-    fillers += [lambda: forward(1)]
-    fillers += [lambda t=t: project(1, t) for t in range(4)]
-    run(reduction(1, factors), fillers, 0.5)
-
-    final = pltpu.make_async_copy(moved1, moved_hbm, store_sem.at[2])
-    final.start()
+    fillers = [
+        (0, lambda: far_tile(1, 3, 1)),
+        (1, lambda: far_tile(1, 3, 2)),
+        (2, lambda: far_tile(1, 3, 3)),
+        (4, lambda: near_item(0, 0)),
+        (5, lambda: near_item(0, 1)),
+        (6, lambda: near_item(0, 2)),
+        (7, lambda: near_item(0, 3)),
+        (8, lambda: query_part(0, [state[0], state[1], state[2]], None, 0)),
+        (9, lambda: query_part(0, [state[0], state[1], state[2]], None, 1)),
+        (9, lambda: share(0)),
+        (9, lambda: near_item(1, 0)),
+        (10, lambda: near_item(1, 1)),
+        (11, lambda: near_item(1, 2)),
+        (12, lambda: near_item(1, 3)),
+        (13, lambda: query_part(1, [moved0[0], moved0[1], moved0[2]], factors, 0)),
+        (14, lambda: query_part(1, [moved0[0], moved0[1], moved0[2]], factors, 1)),
+        (14, lambda: share(1)),
+        (15, lambda: forward(0)),
+        (15, lambda: project(0, 0)),
+        (16, lambda: project(0, 1)),
+        (17, lambda: project(0, 2)),
+        (18, lambda: project(0, 3)),
+        (19, lambda: forward(1)),
+        (19, lambda: project(1, 0)),
+        (20, lambda: project(1, 1)),
+        (21, lambda: project(1, 2)),
+        (22, lambda: project(1, 3)),
+    ]
+    run(reduction(1, factors), fillers)
+
+    finals = [
+        pltpu.make_async_copy(moved1.at[0], up_out.at[0, 0], store_sem.at[2]),
+        pltpu.make_async_copy(moved1.at[1], up_out.at[1, 0], store_sem.at[3]),
+        pltpu.make_async_copy(moved1.at[2], down_out.at[0], store_sem.at[4]),
+    ]
+    for final in finals:
+        final.start()
     for matrix in range(3):
         last = square_sum(moved1[matrix].astype(F32))
         factor = norm[matrix] * lax.rsqrt(last + 1e-06)
         factor_out[matrix] = jnp.broadcast_to(factor, (8, LANES))
     for block in range(BLOCKS):
         for head in range(HEADS):
-            q_copy(block, head).wait_send()
-            o_copy(block, head).wait_send()
+            for tile in range(4):
+                q_copy(block, head, tile).wait_send()
+                o_copy(block, head, tile).wait_send()
         stat_copy(block).wait_send()
         for kind in range(3):
             head_copy(block, kind).wait_send()
         pltpu.make_async_copy(out_stage.at[block], out_hbm.at[block], store_sem.at[block]).wait()
-    final.wait()
+    for final in finals:
+        final.wait()
 
 
 def body(hidden_in, projected, w_out, fast_up, fast_down, learn_rates):
@@ -454,15 +538,16 @@
     hbm_spec = pl.BlockSpec(memory_space=pl.ANY)
     vmem_spec = pl.BlockSpec(memory_space=pltpu.VMEM)
     square = (FD, FD)
-    layer_out, moved, factor = pl.pallas_call(
+    layer_out, up_moved, down_moved, factor = pl.pallas_call(
         layer_kernel,
         out_shape=(
             jax.ShapeDtypeStruct((BLOCKS, TOK, FD), BF16),
-            jax.ShapeDtypeStruct((3, FD, FD), BF16),
+            jax.ShapeDtypeStruct((2, 1, FD, FD), BF16),
+            jax.ShapeDtypeStruct((1, FD, FD), BF16),
             jax.ShapeDtypeStruct((3, 8, LANES), F32),
         ),
         in_specs=[hbm_spec] * 5 + [vmem_spec],
-        out_specs=(hbm_spec, hbm_spec, vmem_spec),
+        out_specs=(hbm_spec, hbm_spec, hbm_spec, vmem_spec),
         scratch_shapes=[
             vmem((3, BLOCKS, TOK, FD), BF16),
             vmem((BLOCKS, TOK, FD), BF16),
@@ -492,11 +577,11 @@
             vmem((BLOCKS, TOK, FD), BF16),
             vmem(square, F32),
             dma((10,)),
-            dma((3,)),
-            dma((8,)),
-            dma((8,)),
-            dma((8,)),
-            dma((8,)),
+            dma((5,)),
+            dma((32,)),
+            dma((32,)),
+            dma((32,)),
+            dma((32,)),
             dma((2,)),
             dma((2,)),
             dma((2, 3)),
@@ -514,8 +599,11 @@
             collective_id=0, has_side_effects=True, vmem_limit_bytes=60 << 20
         ),
     )(hidden_in, projected, w_out, fast_up, fast_down, learn_rates)
-    finals = moved.astype(F32) * factor[:, :1, :1]
-    return (layer_out, finals[:2, None], finals[2:])
+    return (
+        layer_out,
+        up_moved.astype(F32) * factor[:2, None, :1, :1],
+        down_moved.astype(F32) * factor[2:, :1, :1],
+    )
 
 
 def solution(mesh):

time: 157 us -> 137 us (0.87)
  the two profiles are of different devices: /device:TPU:64 before, /device:TPU:1 now
where the time goes in v2:
time: 137 us
  Pallas kernels  128 us (93%)
  other arithmetic  4.76 us (3%)
  local copies, waits for them, and re-layouts  3.02 us (2%)
    pallas_call x1, Pallas kernels, body(): pl.pallas_call(layer_kernel, out_shape=(jax.ShapeDtypeStruct((BLOCKS, TOK...  128 us
    mul x1, other arithmetic, body(): up_moved.astype(F32) * factor[:2, None, :1, :1]  3 us

profile of v2, /device:TPU:1, one launch (start us, length us, event | category | flops | bytes accessed | tf_op | source)
XLA Modules:
  0.0 136.6 jit_solution(4334967335421506268)
XLA Ops:
  0.6 128.2 %shard_map.85 = (bf16[2,512,512]{2,1,0:T(8,128)(2,1)}, bf16[2,1,512,512]{3,2,1,0:T(8,128)(2,1)}, bf16[1,512,512]{2,1,0:T(8,128)(2,1)}, f32[3,8,128]{2,1,0:T(8,128)}) custom-call(bf16[2,512,512]{2,1,0:T(8,128)(2,1)} %hidden_hbm.1, bf16[3,2,512,512]{3,2,1,0:T(8,128)(2,1)} %proj_hbm.1, bf16[2048,512]{1,0:T(8,128)(2,1)} %wout_hbm.1, ...), custom_call_target="tpu_custom_call" | custom-call | tf_op jit(solution)/shard_map/pallas_call | solution.py:541
  128.8 0.0 copy-start.1
  128.8 1.2 slice.7
  130.1 0.8 slice_reduce_fusion
  130.9 0.0 copy-start
  130.9 3.0 %convert_multiply_fusion = f32[2,1,512,512]{3,2,1,0:T(8,128)} fusion(bf16[2,1,512,512]{3,2,1,0:T(8,128)(2,1)} %get-tuple-element.8, f32[2]{0:T(128)S(1)} %slice_reduce_fusion), kind=kLoop, calls=%fused_computation | loop fusion | flops 1048576 | bytes 3145736 | tf_op jit(solution)/shard_map/mul | solution.py:604
  133.9 0.0 copy-done.1
  133.9 1.8 %convert_multiply_fusion.1 = f32[1,512,512]{2,1,0:T(8,128)} fusion(bf16[1,512,512]{2,1,0:T(8,128)(2,1)S(1)} %copy-done.1, f32[]{:T(128)} %bitcast), kind=kLoop, calls=%fused_computation.1 | loop fusion | flops 524288 | bytes 1572868 | tf_op jit(solution)/shard_map/mul | solution.py:605
  135.7 0.0 copy-done
  135.7 1.0 copy.10
Async XLA Ops:
  128.8 5.1 %copy-start.1 = (bf16[1,512,512]{2,1,0:T(8,128)(2,1)S(1)}, bf16[1,512,512]{2,1,0:T(8,128)(2,1)}, u32[]{:S(2)}) copy-start(bf16[1,512,512]{2,1,0:T(8,128)(2,1)} %get-tuple-element.10) | copy-start | bytes 1572868
  130.9 4.8 %copy-start = (bf16[2,512,512]{2,1,0:T(8,128)(2,1)S(1)}, bf16[2,512,512]{2,1,0:T(8,128)(2,1)}, u32[]{:S(2)}) copy-start(bf16[2,512,512]{2,1,0:T(8,128)(2,1)} %get-tuple-element.14) | copy-start | bytes 3145732

commit v3 on v2

--- a/solution.py
+++ b/solution.py
@@ -48,6 +48,8 @@
             "y1": self.at(self.x, self.z, self.y + 1 - 2 * y_low),
             "y3": self.at(self.x, self.z, 3 - self.y),
         }
+        self.along_x = [self.at((self.x + d) % 4, self.z, self.y) for d in (1, 2, 3)]
+        self.along_y = [self.at(self.x, self.z, (self.y + d) % 4) for d in (1, 2, 3)]
         self.z_peer = [self.at(self.x, (self.z + d) % 4, self.y) for d in (1, 2, 3)]
         self.z_to = [(self.z + d) % 4 for d in (1, 2, 3)]
         self.before = ((ctx + 63) % 64, self.head)
@@ -60,9 +62,10 @@
         self.first = ctx == 0
         self.last = ctx // 63
         self.keep, self.send, self.mine = [], [], []
+        self.fan_rows, self.fan_peers = [], []
         for colour in range(COLOURS):
             keeps, sends, off = [], [], 0
-            for step in range(4):
+            for step in range(2):
                 length = 256 >> step
                 key = self.key[ORDER[colour][step]]
                 keeps.append(pl.multiple_of(off + key * length, 32))
@@ -70,7 +73,10 @@
                 off = off + key * length
             self.keep.append(keeps)
             self.send.append(sends)
-            self.mine.append(pl.multiple_of(off, 32))
+            turn = self.y if colour < 2 else self.x
+            self.mine.append(pl.multiple_of(off + turn * 32, 32))
+            self.fan_rows.append([pl.multiple_of(off + (turn + d) % 4 * 32, 32) for d in (1, 2, 3)])
+            self.fan_peers.append(self.along_y if colour < 2 else self.along_x)
 
     def at(self, x, z, y):
         return (x * 16 + z * 4 + y, self.head)
@@ -117,12 +123,12 @@
     hidden_hbm, proj_hbm, wout_hbm, up_hbm, down_hbm, rates,
     out_hbm, up_out, down_out, factor_out,
     proj, hidden, wout, state, q_land, o_out, o_land, stat_out, stat_land, attended, mixed, grad, total, moved0, moved1,
-    land0, land1, land2, land3, z_land, piece, hid, gate_g, up_g, out_g, out_stage, out_acc,
+    land0, land1, fan_land, z_land, piece, hid, gate_g, up_g, out_g, out_stage, out_acc,
     load_sem, store_sem, q_send, q_recv, o_send, o_recv, st_send, st_recv, h_send, h_recv,
-    s_send, s_recv, z_send, z_recv, g_send, g_recv, zg_send, zg_recv,
+    s_send, s_recv, z_send, z_recv, g_send, g_recv, zg_send, zg_recv, fan_send, fan_recv, fg_send, fg_recv,
 ):
     place = Place()
-    lands = (land0, land1, land2, land3)
+    lands = (land0, land1)
     moved = (moved0, moved1)
 
     loads = [
@@ -141,7 +147,7 @@
         load.start()
 
     barrier = pltpu.get_barrier_semaphore()
-    others = list(place.partner.values()) + place.z_peer
+    others = place.along_x + place.along_y + place.z_peer
     others += [place.before, place.after, place.to_sibling, place.to_across]
     for other in others:
         pl.semaphore_signal(barrier, inc=1, device_id=other, device_id_type=MESH)
@@ -181,6 +187,21 @@
             s_send.at[step, matrix, colour],
             s_recv.at[step, matrix, colour],
             place.partner[ORDER[colour][step]],
+        )
+
+    def fan_copy(matrix, colour, d):
+        return remote(
+            block_of(grad, matrix, place.fan_rows[colour][d], 32, colour),
+            fan_land.at[d, matrix, colour],
+            fan_send.at[d, matrix, colour],
+            fan_recv.at[d, matrix, colour],
+            place.fan_peers[colour][d],
+        )
+
+    def fan_gather(block, matrix, colour, d):
+        own = block_of(moved[block], matrix, place.mine[colour], 32, colour)
+        return remote(
+            own, own, fg_send.at[d, matrix, colour], fg_recv.at[d, matrix, colour], place.fan_peers[colour][d]
         )
 
     def z_copy(d, matrix):
@@ -254,7 +275,7 @@
                 scatter_copy(0, matrix, colour).start()
 
     def reduction(block, old_factors):
-        for step in range(4):
+        for step in range(2):
             length = 256 >> step
             for matrix in (2, 1, 0):
                 for colour in range(COLOURS):
@@ -264,12 +285,24 @@
                     value = kept[...] + lands[step][matrix, colour].astype(F32)
                     kept[...] = value
                     block_of(grad, matrix, row, length, colour)[...] = value.astype(BF16)
-                    if step < 3:
-                        scatter_copy(step + 1, matrix, colour).start()
-                if step == 3:
-                    for d in range(3):
-                        z_copy(d, matrix).start()
+                    if step == 0:
+                        scatter_copy(1, matrix, colour).start()
+                    else:
+                        for d in (1, 0, 2):
+                            fan_copy(matrix, colour, d).start()
                 yield
+        for matrix in (2, 1, 0):
+            for colour in range(COLOURS):
+                kept = block_of(total, matrix, place.mine[colour], 32, colour)
+                value = kept[...]
+                for d in range(3):
+                    fan_copy(matrix, colour, d).wait_recv()
+                    value = value + fan_land[d, matrix, colour].astype(F32)
+                kept[...] = value
+                block_of(grad, matrix, place.mine[colour], 32, colour)[...] = value.astype(BF16)
+            for d in range(3):
+                z_copy(d, matrix).start()
+            yield
         for matrix in (2, 1, 0):
             value = block_of(total, matrix, own_row, 32, place.z)[...]
             for d in range(3):
@@ -284,14 +317,21 @@
             for d in range(3):
                 zg_copy(block, d, matrix).start()
             yield
-        for step in (3, 2, 1, 0):
+        for matrix in (2, 1, 0):
+            for d in range(3):
+                zg_copy(block, d, matrix).wait_recv()
+            for d in (1, 0, 2):
+                for colour in range(COLOURS):
+                    fan_gather(block, matrix, colour, d).start()
+            yield
+        for step in (1, 0):
             for matrix in (2, 1, 0):
-                if step == 3:
-                    for d in range(3):
-                        zg_copy(block, d, matrix).wait_recv()
                 for colour in range(COLOURS):
-                    if step < 3:
-                        gather_copy(block, step + 1, matrix, colour).wait_recv()
+                    if step == 1:
+                        for d in range(3):
+                            fan_gather(block, matrix, colour, d).wait_recv()
+                    else:
+                        gather_copy(block, 1, matrix, colour).wait_recv()
                     gather_copy(block, step, matrix, colour).start()
                 yield
         for matrix in (2, 1, 0):
@@ -299,9 +339,12 @@
                 gather_copy(block, 0, matrix, colour).wait_recv()
         for matrix in range(3):
             for colour in range(COLOURS):
-                for step in range(4):
+                for step in range(2):
                     scatter_copy(step, matrix, colour).wait_send()
                     gather_copy(block, step, matrix, colour).wait_send()
+                for d in range(3):
+                    fan_copy(matrix, colour, d).wait_send()
+                    fan_gather(block, matrix, colour, d).wait_send()
             for d in range(3):
                 z_copy(d, matrix).wait_send()
                 zg_copy(block, d, matrix).wait_send()
@@ -416,56 +459,48 @@
         (0, lambda: far_tile(0, 0, 0)),
         (0, lambda: far_tile(0, 0, 1)),
         (0, lambda: far_tile(0, 0, 2)),
+        (0, lambda: far_tile(0, 0, 3)),
         (0, lambda: q_copy(0, 2, 0).start()),
-        (1, lambda: far_tile(0, 0, 3)),
+        (1, lambda: far_tile(0, 1, 0)),
         (1, lambda: q_copy(0, 2, 1).start()),
-        (2, lambda: far_tile(0, 1, 0)),
+        (2, lambda: far_tile(0, 1, 1)),
         (2, lambda: q_copy(0, 2, 2).start()),
-        (3, lambda: far_tile(0, 1, 1)),
+        (3, lambda: far_tile(0, 1, 2)),
         (3, lambda: q_copy(0, 2, 3).start()),
-        (4, lambda: far_tile(0, 1, 2)),
+        (4, lambda: far_tile(0, 1, 3)),
         (4, lambda: q_copy(0, 3, 0).start()),
-        (5, lambda: far_tile(0, 1, 3)),
+        (5, lambda: far_tile(0, 2, 0)),
         (5, lambda: q_copy(0, 3, 1).start()),
-        (6, lambda: far_tile(0, 2, 0)),
+        (6, lambda: far_tile(0, 2, 1)),
         (6, lambda: q_copy(0, 3, 2).start()),
-        (7, lambda: far_tile(0, 2, 1)),
+        (7, lambda: far_tile(0, 2, 2)),
         (7, lambda: q_copy(0, 3, 3).start()),
-        (8, lambda: far_tile(0, 2, 2)),
+        (8, lambda: far_tile(0, 2, 3)),
         (8, lambda: q_copy(1, 0, 0).start()),
-        (9, lambda: far_tile(0, 2, 3)),
+        (9, lambda: far_tile(0, 3, 0)),
         (9, lambda: q_copy(1, 0, 1).start()),
-        (10, lambda: far_tile(0, 3, 0)),
+        (10, lambda: far_tile(0, 3, 1)),
         (10, lambda: q_copy(1, 0, 2).start()),
-        (11, lambda: far_tile(0, 3, 1)),
+        (11, lambda: far_tile(0, 3, 2)),
         (11, lambda: q_copy(1, 0, 3).start()),
-        (12, lambda: far_tile(0, 3, 2)),
+        (12, lambda: far_tile(0, 3, 3)),
         (12, lambda: q_copy(1, 1, 0).start()),
-        (13, lambda: far_tile(0, 3, 3)),
+        (13, lambda: far_tile(1, 0, 0)),
         (13, lambda: q_copy(1, 1, 1).start()),
-        (14, lambda: far_tile(1, 0, 0)),
+        (14, lambda: far_tile(1, 0, 1)),
         (14, lambda: q_copy(1, 1, 2).start()),
-        (15, lambda: far_tile(1, 0, 1)),
+        (15, lambda: far_tile(1, 0, 2)),
         (15, lambda: q_copy(1, 1, 3).start()),
-        (16, lambda: far_tile(1, 0, 2)),
+        (16, lambda: far_tile(1, 0, 3)),
         (16, lambda: q_copy(1, 2, 0).start()),
-        (17, lambda: far_tile(1, 0, 3)),
+        (17, lambda: far_tile(1, 1, 0)),
         (17, lambda: q_copy(1, 2, 1).start()),
-        (18, lambda: far_tile(1, 1, 0)),
+        (18, lambda: far_tile(1, 1, 1)),
         (18, lambda: q_copy(1, 2, 2).start()),
-        (19, lambda: far_tile(1, 1, 1)),
+        (19, lambda: far_tile(1, 1, 2)),
         (19, lambda: q_copy(1, 2, 3).start()),
-        (20, lambda: far_tile(1, 1, 2)),
+        (20, lambda: far_tile(1, 1, 3)),
         (20, lambda: q_copy(1, 3, 0).start()),
-        (21, lambda: far_tile(1, 1, 3)),
-        (21, lambda: q_copy(1, 3, 1).start()),
-        (22, lambda: far_tile(1, 2, 0)),
-        (22, lambda: q_copy(1, 3, 2).start()),
-        (23, lambda: far_tile(1, 2, 1)),
-        (23, lambda: q_copy(1, 3, 3).start()),
-        (24, lambda: far_tile(1, 2, 2)),
-        (25, lambda: far_tile(1, 2, 3)),
-        (26, lambda: far_tile(1, 3, 0)),
     ]
     run(reduction(0, None), fillers)
 
@@ -478,33 +513,41 @@
         norm.append(jnp.sqrt(second) * factors[matrix])
     key_pass(1, [moved0[0], moved0[1], moved0[2]], factors)
     fillers = [
-        (0, lambda: far_tile(1, 3, 1)),
-        (1, lambda: far_tile(1, 3, 2)),
-        (2, lambda: far_tile(1, 3, 3)),
-        (4, lambda: near_item(0, 0)),
+        (0, lambda: far_tile(1, 2, 0)),
+        (0, lambda: q_copy(1, 3, 1).start()),
+        (1, lambda: far_tile(1, 2, 1)),
+        (1, lambda: q_copy(1, 3, 2).start()),
+        (2, lambda: far_tile(1, 2, 2)),
+        (2, lambda: q_copy(1, 3, 3).start()),
+        (3, lambda: far_tile(1, 2, 3)),
+        (4, lambda: far_tile(1, 3, 0)),
+        (5, lambda: far_tile(1, 3, 1)),
+        (5, lambda: near_item(0, 0)),
         (5, lambda: near_item(0, 1)),
+        (6, lambda: far_tile(1, 3, 2)),
         (6, lambda: near_item(0, 2)),
-        (7, lambda: near_item(0, 3)),
-        (8, lambda: query_part(0, [state[0], state[1], state[2]], None, 0)),
-        (9, lambda: query_part(0, [state[0], state[1], state[2]], None, 1)),
-        (9, lambda: share(0)),
+        (6, lambda: near_item(0, 3)),
+        (7, lambda: far_tile(1, 3, 3)),
+        (7, lambda: query_part(0, [state[0], state[1], state[2]], None, 0)),
+        (8, lambda: query_part(0, [state[0], state[1], state[2]], None, 1)),
+        (8, lambda: share(0)),
         (9, lambda: near_item(1, 0)),
-        (10, lambda: near_item(1, 1)),
-        (11, lambda: near_item(1, 2)),
-        (12, lambda: near_item(1, 3)),
-        (13, lambda: query_part(1, [moved0[0], moved0[1], moved0[2]], factors, 0)),
-        (14, lambda: query_part(1, [moved0[0], moved0[1], moved0[2]], factors, 1)),
-        (14, lambda: share(1)),
-        (15, lambda: forward(0)),
-        (15, lambda: project(0, 0)),
-        (16, lambda: project(0, 1)),
-        (17, lambda: project(0, 2)),
-        (18, lambda: project(0, 3)),
-        (19, lambda: forward(1)),
-        (19, lambda: project(1, 0)),
-        (20, lambda: project(1, 1)),
-        (21, lambda: project(1, 2)),
-        (22, lambda: project(1, 3)),
+        (9, lambda: near_item(1, 1)),
+        (10, lambda: near_item(1, 2)),
+        (10, lambda: near_item(1, 3)),
+        (11, lambda: query_part(1, [moved0[0], moved0[1], moved0[2]], factors, 0)),
+        (12, lambda: query_part(1, [moved0[0], moved0[1], moved0[2]], factors, 1)),
+        (12, lambda: share(1)),
+        (12, lambda: forward(0)),
+        (12, lambda: project(0, 0)),
+        (13, lambda: project(0, 1)),
+        (13, lambda: project(0, 2)),
+        (14, lambda: project(0, 3)),
+        (15, lambda: forward(1)),
+        (15, lambda: project(1, 0)),
+        (15, lambda: project(1, 1)),
+        (16, lambda: project(1, 2)),
+        (16, lambda: project(1, 3)),
     ]
     run(reduction(1, factors), fillers)
 
@@ -566,8 +609,7 @@
             vmem((3,) + square, BF16),
             vmem((3, COLOURS, 256, LANES), BF16),
             vmem((3, COLOURS, 128, LANES), BF16),
-            vmem((3, COLOURS, 64, LANES), BF16),
-            vmem((3, COLOURS, 32, LANES), BF16),
+            vmem((3, 3, COLOURS, 32, LANES), BF16),
             vmem((3, 3, 32, LANES), BF16),
             vmem((3, 32, LANES), F32),
             vmem(square, BF16),
@@ -586,14 +628,18 @@
             dma((2,)),
             dma((2, 3)),
             dma((2, 3)),
-            dma((4, 3, COLOURS)),
-            dma((4, 3, COLOURS)),
+            dma((2, 3, COLOURS)),
+            dma((2, 3, COLOURS)),
             dma((3, 3)),
             dma((3, 3)),
-            dma((4, 3, COLOURS)),
-            dma((4, 3, COLOURS)),
+            dma((2, 3, COLOURS)),
+            dma((2, 3, COLOURS)),
             dma((3, 3)),
             dma((3, 3)),
+            dma((3, 3, COLOURS)),
+            dma((3, 3, COLOURS)),
+            dma((3, 3, COLOURS)),
+            dma((3, 3, COLOURS)),
         ],
         compiler_params=pltpu.CompilerParams(
             collective_id=0, has_side_effects=True, vmem_limit_bytes=60 << 20

time: 137 us -> 133 us (0.971)
  Pallas kernels: 128 us -> 123 us
    pallas_call x1, Pallas kernels: 128 us -> 123 us  [body(): pl.pallas_call(layer_kernel, out_shape=(jax.ShapeDtypeStruct((BLOCKS, TOK...]
where the time goes in v3:
time: 133 us; the launch traced here: 132 us
  Pallas kernels  123 us (92%)
  other arithmetic  4.76 us (4%)
  local copies, waits for them, and re-layouts  3.02 us (2%)
    pallas_call x1, Pallas kernels, body(): pl.pallas_call(layer_kernel, out_shape=(jax.ShapeDtypeStruct((BLOCKS, TOK...  123 us
    mul x1, other arithmetic, body(): up_moved.astype(F32) * factor[:2, None, :1, :1]  3 us

profile of v3, /device:TPU:1, one launch (start us, length us, event | category | flops | bytes accessed | tf_op | source)
XLA Modules:
  0.0 131.8 jit_solution(16898786549061512674)
XLA Ops:
  0.6 123.3 %shard_map.85 = (bf16[2,512,512]{2,1,0:T(8,128)(2,1)}, bf16[2,1,512,512]{3,2,1,0:T(8,128)(2,1)}, bf16[1,512,512]{2,1,0:T(8,128)(2,1)}, f32[3,8,128]{2,1,0:T(8,128)}) custom-call(bf16[2,512,512]{2,1,0:T(8,128)(2,1)} %hidden_hbm.1, bf16[3,2,512,512]{3,2,1,0:T(8,128)(2,1)} %proj_hbm.1, bf16[2048,512]{1,0:T(8,128)(2,1)} %wout_hbm.1, ...), custom_call_target="tpu_custom_call" | custom-call | tf_op jit(solution)/shard_map/pallas_call | solution.py:584
  124.0 0.0 copy-start.1
  124.0 1.2 slice.7
  125.2 0.8 slice_reduce_fusion
  126.0 0.0 copy-start
  126.0 3.0 %convert_multiply_fusion = f32[2,1,512,512]{3,2,1,0:T(8,128)} fusion(bf16[2,1,512,512]{3,2,1,0:T(8,128)(2,1)} %get-tuple-element.8, f32[2]{0:T(128)S(1)} %slice_reduce_fusion), kind=kLoop, calls=%fused_computation | loop fusion | flops 1048576 | bytes 3145736 | tf_op jit(solution)/shard_map/mul | solution.py:650
  129.0 0.0 copy-done.1
  129.0 1.8 %convert_multiply_fusion.1 = f32[1,512,512]{2,1,0:T(8,128)} fusion(bf16[1,512,512]{2,1,0:T(8,128)(2,1)S(1)} %copy-done.1, f32[]{:T(128)} %bitcast), kind=kLoop, calls=%fused_computation.1 | loop fusion | flops 524288 | bytes 1572868 | tf_op jit(solution)/shard_map/mul | solution.py:651
  130.8 0.0 copy-done
  130.8 1.0 copy.10
Async XLA Ops:
  124.0 5.1 %copy-start.1 = (bf16[1,512,512]{2,1,0:T(8,128)(2,1)S(1)}, bf16[1,512,512]{2,1,0:T(8,128)(2,1)}, u32[]{:S(2)}) copy-start(bf16[1,512,512]{2,1,0:T(8,128)(2,1)} %get-tuple-element.10) | copy-start | bytes 1572868
  126.0 4.8 %copy-start = (bf16[2,512,512]{2,1,0:T(8,128)(2,1)S(1)}, bf16[2,512,512]{2,1,0:T(8,128)(2,1)}, u32[]{:S(2)}) copy-start(bf16[2,512,512]{2,1,0:T(8,128)(2,1)} %get-tuple-element.14) | copy-start | bytes 3145732

commit v4 on v3

--- a/solution.py
+++ b/solution.py
@@ -460,46 +460,47 @@
         (0, lambda: far_tile(0, 0, 1)),
         (0, lambda: far_tile(0, 0, 2)),
         (0, lambda: far_tile(0, 0, 3)),
+        (0, lambda: far_tile(0, 1, 0)),
         (0, lambda: q_copy(0, 2, 0).start()),
-        (1, lambda: far_tile(0, 1, 0)),
+        (1, lambda: far_tile(0, 1, 1)),
         (1, lambda: q_copy(0, 2, 1).start()),
-        (2, lambda: far_tile(0, 1, 1)),
+        (2, lambda: far_tile(0, 1, 2)),
         (2, lambda: q_copy(0, 2, 2).start()),
-        (3, lambda: far_tile(0, 1, 2)),
+        (3, lambda: far_tile(0, 1, 3)),
         (3, lambda: q_copy(0, 2, 3).start()),
-        (4, lambda: far_tile(0, 1, 3)),
+        (4, lambda: far_tile(0, 2, 0)),
         (4, lambda: q_copy(0, 3, 0).start()),
-        (5, lambda: far_tile(0, 2, 0)),
+        (5, lambda: far_tile(0, 2, 1)),
         (5, lambda: q_copy(0, 3, 1).start()),
-        (6, lambda: far_tile(0, 2, 1)),
+        (6, lambda: far_tile(0, 2, 2)),
         (6, lambda: q_copy(0, 3, 2).start()),
-        (7, lambda: far_tile(0, 2, 2)),
+        (7, lambda: far_tile(0, 2, 3)),
         (7, lambda: q_copy(0, 3, 3).start()),
-        (8, lambda: far_tile(0, 2, 3)),
+        (8, lambda: far_tile(0, 3, 0)),
         (8, lambda: q_copy(1, 0, 0).start()),
-        (9, lambda: far_tile(0, 3, 0)),
+        (9, lambda: far_tile(0, 3, 1)),
         (9, lambda: q_copy(1, 0, 1).start()),
-        (10, lambda: far_tile(0, 3, 1)),
+        (10, lambda: far_tile(0, 3, 2)),
         (10, lambda: q_copy(1, 0, 2).start()),
-        (11, lambda: far_tile(0, 3, 2)),
+        (11, lambda: far_tile(0, 3, 3)),
         (11, lambda: q_copy(1, 0, 3).start()),
-        (12, lambda: far_tile(0, 3, 3)),
+        (12, lambda: far_tile(1, 0, 0)),
         (12, lambda: q_copy(1, 1, 0).start()),
-        (13, lambda: far_tile(1, 0, 0)),
+        (13, lambda: far_tile(1, 0, 1)),
         (13, lambda: q_copy(1, 1, 1).start()),
-        (14, lambda: far_tile(1, 0, 1)),
+        (14, lambda: far_tile(1, 0, 2)),
         (14, lambda: q_copy(1, 1, 2).start()),
-        (15, lambda: far_tile(1, 0, 2)),
+        (15, lambda: far_tile(1, 0, 3)),
         (15, lambda: q_copy(1, 1, 3).start()),
-        (16, lambda: far_tile(1, 0, 3)),
+        (16, lambda: far_tile(1, 1, 0)),
         (16, lambda: q_copy(1, 2, 0).start()),
-        (17, lambda: far_tile(1, 1, 0)),
+        (17, lambda: far_tile(1, 1, 1)),
         (17, lambda: q_copy(1, 2, 1).start()),
-        (18, lambda: far_tile(1, 1, 1)),
+        (18, lambda: far_tile(1, 1, 2)),
         (18, lambda: q_copy(1, 2, 2).start()),
-        (19, lambda: far_tile(1, 1, 2)),
+        (19, lambda: far_tile(1, 1, 3)),
         (19, lambda: q_copy(1, 2, 3).start()),
-        (20, lambda: far_tile(1, 1, 3)),
+        (20, lambda: far_tile(1, 2, 0)),
         (20, lambda: q_copy(1, 3, 0).start()),
     ]
     run(reduction(0, None), fillers)
@@ -513,41 +514,40 @@
         norm.append(jnp.sqrt(second) * factors[matrix])
     key_pass(1, [moved0[0], moved0[1], moved0[2]], factors)
     fillers = [
-        (0, lambda: far_tile(1, 2, 0)),
+        (0, lambda: far_tile(1, 2, 1)),
         (0, lambda: q_copy(1, 3, 1).start()),
-        (1, lambda: far_tile(1, 2, 1)),
+        (1, lambda: far_tile(1, 2, 2)),
         (1, lambda: q_copy(1, 3, 2).start()),
-        (2, lambda: far_tile(1, 2, 2)),
+        (2, lambda: far_tile(1, 2, 3)),
         (2, lambda: q_copy(1, 3, 3).start()),
-        (3, lambda: far_tile(1, 2, 3)),
-        (4, lambda: far_tile(1, 3, 0)),
-        (5, lambda: far_tile(1, 3, 1)),
-        (5, lambda: near_item(0, 0)),
-        (5, lambda: near_item(0, 1)),
-        (6, lambda: far_tile(1, 3, 2)),
-        (6, lambda: near_item(0, 2)),
-        (6, lambda: near_item(0, 3)),
-        (7, lambda: far_tile(1, 3, 3)),
-        (7, lambda: query_part(0, [state[0], state[1], state[2]], None, 0)),
-        (8, lambda: query_part(0, [state[0], state[1], state[2]], None, 1)),
-        (8, lambda: share(0)),
-        (9, lambda: near_item(1, 0)),
-        (9, lambda: near_item(1, 1)),
-        (10, lambda: near_item(1, 2)),
-        (10, lambda: near_item(1, 3)),
-        (11, lambda: query_part(1, [moved0[0], moved0[1], moved0[2]], factors, 0)),
-        (12, lambda: query_part(1, [moved0[0], moved0[1], moved0[2]], factors, 1)),
-        (12, lambda: share(1)),
-        (12, lambda: forward(0)),
-        (12, lambda: project(0, 0)),
-        (13, lambda: project(0, 1)),
-        (13, lambda: project(0, 2)),
-        (14, lambda: project(0, 3)),
-        (15, lambda: forward(1)),
-        (15, lambda: project(1, 0)),
-        (15, lambda: project(1, 1)),
-        (16, lambda: project(1, 2)),
-        (16, lambda: project(1, 3)),
+        (3, lambda: far_tile(1, 3, 0)),
+        (4, lambda: far_tile(1, 3, 1)),
+        (4, lambda: near_item(0, 0)),
+        (4, lambda: near_item(0, 1)),
+        (5, lambda: far_tile(1, 3, 2)),
+        (5, lambda: near_item(0, 2)),
+        (5, lambda: near_item(0, 3)),
+        (6, lambda: far_tile(1, 3, 3)),
+        (6, lambda: query_part(0, [state[0], state[1], state[2]], None, 0)),
+        (7, lambda: query_part(0, [state[0], state[1], state[2]], None, 1)),
+        (7, lambda: share(0)),
+        (8, lambda: near_item(1, 0)),
+        (8, lambda: near_item(1, 1)),
+        (9, lambda: near_item(1, 2)),
+        (9, lambda: near_item(1, 3)),
+        (10, lambda: query_part(1, [moved0[0], moved0[1], moved0[2]], factors, 0)),
+        (11, lambda: query_part(1, [moved0[0], moved0[1], moved0[2]], factors, 1)),
+        (11, lambda: share(1)),
+        (11, lambda: forward(0)),
+        (11, lambda: project(0, 0)),
+        (12, lambda: project(0, 1)),
+        (12, lambda: project(0, 2)),
+        (13, lambda: project(0, 3)),
+        (14, lambda: forward(1)),
+        (14, lambda: project(1, 0)),
+        (14, lambda: project(1, 1)),
+        (15, lambda: project(1, 2)),
+        (15, lambda: project(1, 3)),
     ]
     run(reduction(1, factors), fillers)
 

time: 133 us -> 137 us (1.030)
  Pallas kernels: 123 us -> 128 us
    pallas_call x1, Pallas kernels: 123 us -> 128 us  [body(): pl.pallas_call(layer_kernel, out_shape=(jax.ShapeDtypeStruct((BLOCKS, TOK...]
where the time goes in v4:
time: 137 us
  Pallas kernels  128 us (93%)
  other arithmetic  4.76 us (3%)
  local copies, waits for them, and re-layouts  3.02 us (2%)
    pallas_call x1, Pallas kernels, body(): pl.pallas_call(layer_kernel, out_shape=(jax.ShapeDtypeStruct((BLOCKS, TOK...  128 us
    mul x1, other arithmetic, body(): up_moved.astype(F32) * factor[:2, None, :1, :1]  3 us

profile of v4, /device:TPU:1, one launch (start us, length us, event | category | flops | bytes accessed | tf_op | source)
XLA Modules:
  0.0 136.5 jit_solution(12835229353319988064)
XLA Ops:
  0.6 128.1 %shard_map.85 = (bf16[2,512,512]{2,1,0:T(8,128)(2,1)}, bf16[2,1,512,512]{3,2,1,0:T(8,128)(2,1)}, bf16[1,512,512]{2,1,0:T(8,128)(2,1)}, f32[3,8,128]{2,1,0:T(8,128)}) custom-call(bf16[2,512,512]{2,1,0:T(8,128)(2,1)} %hidden_hbm.1, bf16[3,2,512,512]{3,2,1,0:T(8,128)(2,1)} %proj_hbm.1, bf16[2048,512]{1,0:T(8,128)(2,1)} %wout_hbm.1, ...), custom_call_target="tpu_custom_call" | custom-call | tf_op jit(solution)/shard_map/pallas_call | solution.py:584
  128.7 0.0 copy-start.1
  128.8 1.2 slice.7
  130.0 0.8 slice_reduce_fusion
  130.8 0.0 copy-start
  130.8 3.0 %convert_multiply_fusion = f32[2,1,512,512]{3,2,1,0:T(8,128)} fusion(bf16[2,1,512,512]{3,2,1,0:T(8,128)(2,1)} %get-tuple-element.8, f32[2]{0:T(128)S(1)} %slice_reduce_fusion), kind=kLoop, calls=%fused_computation | loop fusion | flops 1048576 | bytes 3145736 | tf_op jit(solution)/shard_map/mul | solution.py:650
  133.8 0.0 copy-done.1
  133.8 1.8 %convert_multiply_fusion.1 = f32[1,512,512]{2,1,0:T(8,128)} fusion(bf16[1,512,512]{2,1,0:T(8,128)(2,1)S(1)} %copy-done.1, f32[]{:T(128)} %bitcast), kind=kLoop, calls=%fused_computation.1 | loop fusion | flops 524288 | bytes 1572868 | tf_op jit(solution)/shard_map/mul | solution.py:651
  135.6 0.0 copy-done
  135.6 1.0 copy.10
Async XLA Ops:
  128.7 5.1 %copy-start.1 = (bf16[1,512,512]{2,1,0:T(8,128)(2,1)S(1)}, bf16[1,512,512]{2,1,0:T(8,128)(2,1)}, u32[]{:S(2)}) copy-start(bf16[1,512,512]{2,1,0:T(8,128)(2,1)} %get-tuple-element.10) | copy-start | bytes 1572868
  130.8 4.8 %copy-start = (bf16[2,512,512]{2,1,0:T(8,128)(2,1)S(1)}, bf16[2,512,512]{2,1,0:T(8,128)(2,1)}, u32[]{:S(2)}) copy-start(bf16[2,512,512]{2,1,0:T(8,128)(2,1)} %get-tuple-element.14) | copy-start | bytes 3145732
